TPU v7x, 32 devices: a whole 2x2x4 slice. The times are simulated.
32 devices in a mesh: gx: 16 (over z, x, core), gy: 2 (over y).
Axes of the slice: x: 2, y: 2, z: 4, core: 2. Of those that a mesh axis runs over, the one named last changes fastest.
Arguments:
- flexibility: bfloat16 [16, 2, 2048, 2048], P('gx', 'gy'), may hold values from -8 to 8
- loads: bfloat16 [16, 2, 192, 2048], P('gx', 'gy'), may hold values from -30 to 30
- dof_order: int32 [16, 2, 2048], P('gx', 'gy'), may hold values from 0 to 2047, each once within a row
- coarse_ids: int32 [16, 2, 128], P('gx', 'gy'), may hold values from 0 to 127, each once within a row
Outputs:
- field: float32 [16, 2, 192, 2048], P('gx', 'gy')
- multipliers: float32 [16, 2, 192, 2048], P('gx', 'gy')
All inputs are finite; a program needn't handle non-finite values.
Results may differ from a plain program's by a relative error of at most 0.0038.
Values may be sent and summed in bfloat16 or wider, within the bound.
A program may use at most 64 MiB of HBM per device.

v0:
```python
import jax
import jax.numpy as jnp
from jax import lax
from jax.sharding import PartitionSpec as P

ITERS = 2


RHO = 0.2
RHO_CORNER = 0.5
EPS = 1e-06


def shifted(block, axis, distance):
    devices = range(lax.axis_size(axis))
    route = [((i - distance) % len(devices), i) for i in devices]
    return lax.ppermute(block, axis, route)


def passed_along(array, axis, by):
    size = lax.axis_size(axis)
    pairs = [(i, i + by) for i in range(size) if 0 <= i + by < size]
    return lax.ppermute(array, axis, pairs)


def split_pair(faces, position, dist, first, second):
    odd = position // dist % 2 == 1
    send_up = jnp.where(odd, faces[second], faces[first])
    send_down = jnp.where(odd, faces[first], faces[second])
    return (odd, send_up, send_down)


def place(partners, odd, below, above, first, second):
    partners[first] = jnp.where(odd, below, above)
    partners[second] = jnp.where(odd, above, below)


def local(flexibility, loads, dof_order, coarse_ids):
    flex = flexibility[0, 0]
    load = loads[0, 0].astype(jnp.float32)
    order = dof_order[0, 0]
    ids = coarse_ids[0, 0]
    slot_inverse = jnp.argsort(ids)
    rhs_count, order_count = load.shape
    corner_count = ids.shape[0]
    per_cross = corner_count // 4
    face = (order_count - corner_count) // 6
    length_count = lax.axis_size("gx")
    entries = length_count * lax.axis_size("gy") * corner_count
    index_x = lax.axis_index("gx")
    index_y = lax.axis_index("gy")
    multipliers = jnp.zeros((rhs_count, order_count), jnp.float32)
    field = multipliers
    for step in range(ITERS):
        rhs = (load - multipliers).astype(jnp.bfloat16)
        field = jnp.dot(rhs, flex, preferred_element_type=jnp.float32)
        ordered = jnp.take(field, order, axis=1)
        traces = ordered[:, : 6 * face].astype(jnp.bfloat16)
        faces = [traces[:, r * face : (r + 1) * face] for r in range(6)]
        corners = ordered[:, 6 * face :]
        slotted = jnp.transpose(
            jnp.take(corners, slot_inverse, axis=1).reshape(rhs_count, 4, per_cross), (1, 0, 2)
        )
        partners = [None] * 6
        odd_y, up_y, down_y = split_pair(faces, index_y, 1, 2, 3)
        below_y = shifted(up_y, "gy", 1)
        above_y = shifted(down_y, "gy", -1)
        raised = shifted(slotted[2:], "gy", -1)
        place(partners, odd_y, below_y, above_y, 2, 3)
        upper = slotted[0] + raised[0]
        lower = slotted[1] + raised[1]
        odd_x, up_x, down_x = split_pair(faces, index_x, 1, 0, 1)
        below_x = passed_along(up_x, "gx", 1)
        above_x = passed_along(down_x, "gx", -1)
        later = passed_along(lower, "gx", -1)
        place(partners, odd_x, below_x, above_x, 0, 1)
        odd_f, up_f, down_f = split_pair(faces, index_x, 2, 4, 5)
        below_f = passed_along(up_f, "gx", 2)
        above_f = passed_along(down_f, "gx", -2)
        place(partners, odd_f, below_f, above_f, 4, 5)
        cross = upper + later
        count = jnp.where(index_x == length_count - 1, 2.0, 4.0).astype(jnp.float32)
        own_mean = cross / count
        edge_mean = lower * 0.5
        squares = jnp.sum(corners * corners, axis=1)
        owned = count * jnp.sum(own_mean * own_mean, axis=1)
        edge_part = jnp.where(index_x == 0, 2.0 * jnp.sum(edge_mean * edge_mean, axis=1), 0.0)
        total_sq = lax.psum(squares - owned - edge_part, ("gx", "gy"))
        back_x = passed_along(own_mean, "gx", 1)
        slot_b = jnp.where(index_x == 0, edge_mean, back_x)
        back_y = shifted(jnp.stack([own_mean, slot_b]), "gy", 1)
        means = jnp.stack([own_mean, slot_b, back_y[0], back_y[1]])
        averaged = jnp.transpose(means, (1, 0, 2)).reshape(rhs_count, corner_count)
        average = jnp.take(averaged, ids, axis=1)
        resid = corners - average
        scale = 1.0 / jnp.sqrt(total_sq / entries + EPS)
        pieces = []
        for r in range(6):
            own = ordered[:, r * face : (r + 1) * face]
            pieces.append(RHO * (own - partners[r].astype(jnp.float32)))
        pieces.append(RHO_CORNER * resid * scale[:, None])
        update = jnp.concatenate(pieces, axis=1)
        multipliers = multipliers + jnp.zeros_like(update).at[:, order].set(update)
    return (field[None, None], multipliers[None, None])


def solution(mesh):
    placed = (
        P("gx", "gy", None, None),
        P("gx", "gy", None, None),
        P("gx", "gy", None),
        P("gx", "gy", None),
    )
    return jax.shard_map(
        local,
        mesh=mesh,
        in_specs=placed,
        out_specs=(P("gx", "gy", None, None), P("gx", "gy", None, None)),
        check_vma=False,
    )
```

profile of v0, /device:TPU:0, one launch (start us, length us, event | category | flops | bytes accessed | tf_op | source)
XLA Modules:
  0.0 225.9 jit_solution(10532208125408013064)
XLA Ops:
  0.6 0.7 fusion.48
  1.3 0.7 compare_and_fusion
  2.0 7.0 %fusion.2 = f32[192,2048]{0,1:T(8,128)S(1)} fusion(bf16[1,1,2048,2048]{3,2,1,0:T(8,128)(2,1)} %param.8, bf16[1,1,192,2048]{3,2,1,0:T(8,128)(2,1)} %param.9), kind=kOutput, calls=%fused_computation.10 | convolution fusion | flops 1610612736 | bytes 10747904 | tf_op jit(solution)/shard_map/dot_general | solution.py:56
  9.1 8.6 %gather_fusion = f32[2048,192]{1,0:T(8,128)} fusion(f32[192,2048]{0,1:T(8,128)S(1)} %fusion.2, s32[2048]{0:T(1024)S(1)} %fusion.48), kind=kCustom, calls=%fused_computation.clone | custom fusion | bytes 3153920 | tf_op jit(solution)/shard_map/jit(_take)/gather | solution.py:57
  17.6 1.8 fusion.54
  19.4 1.0 broadcast_select_fusion.2
  20.4 3.0 %collective-permute-start = (bf16[192,320]{0,1:T(8,128)(2,1)}, bf16[192,320]{0,1:T(8,128)(2,1)}, u32[]{:S(2)}, u32[]{:S(2)}) collective-permute-start(bf16[192,320]{0,1:T(8,128)(2,1)} %get-tuple-element.35), channel_id=1, source_target_pairs={{0,2},{2,4},{4,6},{6,8},{8,10},{10,12},{12,14},{14,16},{16,18},{18... | collective-permute-start | bytes 368648 | tf_op jit(solution)/shard_map/ppermute | solution.py:23
  23.4 1.3 collective-permute-start.1
  24.7 2.4 %collective-permute-start.2 = (bf16[192,320]{0,1:T(8,128)(2,1)}, bf16[192,320]{0,1:T(8,128)(2,1)S(1)}, u32[]{:S(2)}, u32[]{:S(2)}) collective-permute-start(bf16[192,320]{0,1:T(8,128)(2,1)} %get-tuple-element.33), channel_id=1, source_target_pairs={{1,0},{0,1},{3,2},{2,3},{5,4},{4,5},{7,6},{6,7},{9,8},{8,9},{11,10... | collective-permute-start | bytes 368648 | tf_op jit(solution)/shard_map/ppermute | solution.py:17
  27.2 2.5 %sort.17 = (s32[128]{0:T(128)}, s32[128]{0:T(128)S(1)}) sort(s32[128]{0:T(128)S(1)} %bitcast.107, s32[128]{0:T(128)S(1)} %iota.4), dimensions={0}, to_apply=%region_0.2 | sort | flops 896 | bytes 2048 | tf_op jit(solution)/shard_map/jit(argsort)/sort | solution.py:43
  29.7 0.6 multiply_reduce_fusion.1
  30.3 0.8 gather_fusion.1
  31.2 2.0 collective-permute-start.6
  33.2 0.6 compare_select_fusion
  33.8 0.6 compare_and_fusion.1
  34.4 1.9 collective-permute-done.6
  36.3 0.6 multiply_reduce_fusion.4
  36.9 1.3 collective-permute-start.7
  38.2 1.4 copy.10
  39.7 0.8 collective-permute-done.7
  40.5 0.8 multiply_reduce_fusion.5
  41.3 6.5 %collective-permute-start.8 = (f32[192,32]{0,1:T(8,128)S(1)}, f32[192,32]{0,1:T(8,128)}, u32[]{:S(2)}, u32[]{:S(2)}) collective-permute-start(f32[192,32]{0,1:T(8,128)S(1)} %get-tuple-element.17), channel_id=1, source_target_pairs={{0,2},{2,4},{4,6},{6,8},{8,10},{10,12},{12,14},{14,16},{16,18},{18... | collective-permute-start | bytes 73736 | tf_op jit(solution)/shard_map/ppermute | solution.py:23
  47.8 1.2 select_subtract_fusion.1
  49.0 40.2 %psum.14 = f32[192]{0:T(256)} all-reduce(f32[192]{0:T(256)} %select_subtract_fusion.1), channel_id=1, replica_groups=mesh['gx'=16,'gy'=2] {'gx','gy'}, use_global_device_ids=true, to_apply=%region_4.7 | all-reduce | flops 192 | bytes 1536 | tf_op jit(solution)/shard_map/psum | solution.py:88
  89.2 1.2 rsqrt_multiply_fusion.1
  90.5 4.2 %collective-permute-start.4 = (bf16[192,320]{0,1:T(8,128)(2,1)}, bf16[192,320]{0,1:T(8,128)(2,1)S(1)}, u32[]{:S(2)}, u32[]{:S(2)}) collective-permute-start(bf16[192,320]{0,1:T(8,128)(2,1)} %get-tuple-element.37), channel_id=1, source_target_pairs={{0,4},{2,6},{4,8},{6,10},{8,12},{10,14},{12,16},{14,18},{16,20},{1... | collective-permute-start | bytes 368648 | tf_op jit(solution)/shard_map/ppermute | solution.py:23
  94.7 1.3 collective-permute-start.5
  96.0 0.8 collective-permute-start.9
  96.9 1.0 fusion.35
  97.9 1.0 fusion.33
  99.0 0.6 collective-permute-done.4
  99.6 2.6 %collective-permute-done.5 = bf16[192,320]{0,1:T(8,128)(2,1)S(1)} collective-permute-done((bf16[192,320]{0,1:T(8,128)(2,1)}, bf16[192,320]{0,1:T(8,128)(2,1)S(1)}, u32[]{:S(2)}, u32[]{:S(2)}) %collective-permute-start.5) | collective-permute-done | bytes 122912 | tf_op jit(solution)/shard_map/ppermute | solution.py:23
  102.3 1.3 copy-done.3
  103.7 0.8 gather_fusion.2
  104.5 0.7 fusion.39
  105.2 10.3 %scatter_custom_fusion = f32[192,2048]{0,1:T(8,128)S(1)} fusion(s32[2048]{0:T(1024)} %bitcast.105, f32[192,2048]{0,1:T(8,128)} %fusion.39, f32[]{:T(128)} %constant.99.clone.1), kind=kCustom, calls=%fused_computation.14 | custom fusion | bytes 3670528 | tf_op jit(solution)/shard_map/scatter | solution.py:103
  115.5 1.3 copy-done
  116.8 6.4 %fusion = f32[192,2048]{1,0:T(8,128)} fusion(bf16[1,1,2048,2048]{3,2,1,0:T(8,128)(2,1)} %param.8, f32[192,2048]{0,1:T(8,128)S(1)} %scatter_custom_fusion, bf16[1,1,192,2048]{2,3,1,0:T(8,128)(2,1)S(1)} %copy.10), kind=kOutput, calls=%fused_computation.8 | convolution fusion | flops 1611792384 | bytes 12320768 | tf_op jit(solution)/shard_map/dot_general | solution.py:56
  123.2 1.8 copy.12
  125.0 8.6 %gather_fusion.3 = f32[2048,192]{1,0:T(8,128)} fusion(f32[192,2048]{0,1:T(8,128)S(1)} %copy.12, s32[2048]{0:T(1024)S(1)} %fusion.48), kind=kCustom, calls=%fused_computation.2.clone | custom fusion | bytes 3153920 | tf_op jit(solution)/shard_map/jit(_take)/gather | solution.py:57
  133.6 1.8 fusion.51
  135.4 0.9 gather_fusion.4
  136.3 0.1 broadcast_select_fusion.12
  136.4 1.2 collective-permute-start.16
  137.5 3.2 %collective-permute-done.16 = f32[2,192,32]{1,2,0:T(8,128)S(1)} collective-permute-done((f32[2,192,32]{1,2,0:T(8,128)S(1)}, f32[2,192,32]{1,2,0:T(8,128)S(1)}, u32[]{:S(2)}, u32[]{:S(2)}) %collective-permute-start.16) | collective-permute-done | bytes 49184 | tf_op jit(solution)/shard_map/ppermute | solution.py:17
  140.7 1.3 collective-permute-start.17
  142.0 0.9 broadcast_select_fusion
  143.0 3.0 %collective-permute-start.10 = (bf16[192,320]{0,1:T(8,128)(2,1)}, bf16[192,320]{0,1:T(8,128)(2,1)S(1)}, u32[]{:S(2)}, u32[]{:S(2)}) collective-permute-start(bf16[192,320]{0,1:T(8,128)(2,1)} %get-tuple-element.29), channel_id=1, source_target_pairs={{0,2},{2,4},{4,6},{6,8},{8,10},{10,12},{12,14},{14,16},{16,18},{18... | collective-permute-start | bytes 368648 | tf_op jit(solution)/shard_map/ppermute | solution.py:23
  146.0 1.3 collective-permute-start.11
  147.3 1.2 collective-permute-start.12
  148.4 0.9 collective-permute-start.13
  149.4 3.5 %collective-permute-start.18 = (f32[192,32]{0,1:T(8,128)S(1)}, f32[192,32]{0,1:T(8,128)S(1)}, u32[]{:S(2)}, u32[]{:S(2)}) collective-permute-start(f32[192,32]{0,1:T(8,128)S(1)} %get-tuple-element.11), channel_id=1, source_target_pairs={{0,2},{2,4},{4,6},{6,8},{8,10},{10,12},{12,14},{14,16},{16,18},{18... | collective-permute-start | bytes 73736 | tf_op jit(solution)/shard_map/ppermute | solution.py:23
  153.0 41.5 %psum.15 = f32[192]{0:T(256)S(1)} all-reduce(f32[192]{0:T(256)S(1)} %select_subtract_fusion), channel_id=1, replica_groups=mesh['gx'=16,'gy'=2] {'gx','gy'}, use_global_device_ids=true, to_apply=%region_9.12 | all-reduce | flops 192 | bytes 1536 | tf_op jit(solution)/shard_map/psum | solution.py:88
  194.4 4.2 %collective-permute-start.14 = (bf16[192,320]{0,1:T(8,128)(2,1)}, bf16[192,320]{0,1:T(8,128)(2,1)S(1)}, u32[]{:S(2)}, u32[]{:S(2)}) collective-permute-start(bf16[192,320]{0,1:T(8,128)(2,1)} %get-tuple-element.31), channel_id=1, source_target_pairs={{0,4},{2,6},{4,8},{6,10},{8,12},{10,14},{12,16},{14,18},{16,20},{1... | collective-permute-start | bytes 368648 | tf_op jit(solution)/shard_map/ppermute | solution.py:23
  198.7 1.3 collective-permute-start.15
  200.0 1.8 collective-permute-start.19
  202.0 3.3 %collective-permute-done.14 = bf16[192,320]{0,1:T(8,128)(2,1)S(1)} collective-permute-done((bf16[192,320]{0,1:T(8,128)(2,1)}, bf16[192,320]{0,1:T(8,128)(2,1)S(1)}, u32[]{:S(2)}, u32[]{:S(2)}) %collective-permute-start.14) | collective-permute-done | bytes 122912 | tf_op jit(solution)/shard_map/ppermute | solution.py:23
  205.3 0.6 collective-permute-done.15
  206.0 1.3 copy-done.2
  207.4 0.8 gather_fusion.5
  208.1 0.7 fusion.37
  208.9 11.1 %scatter_custom_fusion.1 = f32[192,2048]{0,1:T(8,128)} fusion(s32[2048]{0:T(1024)} %bitcast.106, f32[192,2048]{0,1:T(8,128)} %fusion.37, f32[]{:T(128)} %constant.99.clone.1), kind=kCustom, calls=%fused_computation.12 | custom fusion | bytes 3670528 | tf_op jit(solution)/shard_map/scatter | solution.py:103
  220.0 3.2 %add_bitcast_fusion = f32[1,1,192,2048]{2,3,1,0:T(8,128)} fusion(f32[192,2048]{0,1:T(8,128)S(1)} %copy-done.1, f32[192,2048]{0,1:T(8,128)} %scatter_custom_fusion.1), kind=kLoop, calls=%fused_computation.18 | loop fusion | flops 393216 | bytes 4718592 | tf_op jit(solution)/shard_map/broadcast_in_dim | solution.py:104
  223.1 2.8 %copy.13 = f32[1,1,192,2048]{3,2,1,0:T(8,128)} copy(f32[1,1,192,2048]{2,3,1,0:T(8,128)} %add_bitcast_fusion) | data formatting | bytes 3145728
  (67 shorter events, 1.1 us)
Async XLA Ops:
  17.6 9.6 %copy-start.12 = (s32[1,1,128]{2,1,0:T(1,128)S(1)}, s32[1,1,128]{2,1,0:T(1,128)}, u32[]{:S(2)}) copy-start(s32[1,1,128]{2,1,0:T(1,128)} %param.11) | copy-start | bytes 1540
  19.4 13.8 %copy-start.5 = (s32[1,1,2048]{2,1,0:T(1,128)S(1)}, s32[1,1,2048]{2,1,0:T(1,128)}, u32[]{:S(2)}) copy-start(s32[1,1,2048]{2,1,0:T(1,128)} %param.10) | copy-start | bytes 24580
  20.4 74.3 %collective-permute-start = (bf16[192,320]{0,1:T(8,128)(2,1)}, bf16[192,320]{0,1:T(8,128)(2,1)}, u32[]{:S(2)}, u32[]{:S(2)}) collective-permute-start(bf16[192,320]{0,1:T(8,128)(2,1)} %get-tuple-element.35), channel_id=1, source_target_pairs={{0,2},{2,4},{4,6},{6,8},{8,10},{10,12},{12,14},{14,16},{16,18},{18... | collective-permute-start | bytes 368648 | tf_op jit(solution)/shard_map/ppermute | solution.py:23
  23.4 72.6 %collective-permute-start.1 = (bf16[192,320]{0,1:T(8,128)(2,1)}, bf16[192,320]{0,1:T(8,128)(2,1)}, u32[]{:S(2)}, u32[]{:S(2)}) collective-permute-start(bf16[192,320]{0,1:T(8,128)(2,1)} %get-tuple-element.36), channel_id=1, source_target_pairs={{2,0},{4,2},{6,4},{8,6},{10,8},{12,10},{14,12},{16,14},{18,16},{20... | collective-permute-start | bytes 368648 | tf_op jit(solution)/shard_map/ppermute | solution.py:23
  24.7 74.1 %collective-permute-start.2 = (bf16[192,320]{0,1:T(8,128)(2,1)}, bf16[192,320]{0,1:T(8,128)(2,1)S(1)}, u32[]{:S(2)}, u32[]{:S(2)}) collective-permute-start(bf16[192,320]{0,1:T(8,128)(2,1)} %get-tuple-element.33), channel_id=1, source_target_pairs={{1,0},{0,1},{3,2},{2,3},{5,4},{4,5},{7,6},{6,7},{9,8},{8,9},{11,10... | collective-permute-start | bytes 368648 | tf_op jit(solution)/shard_map/ppermute | solution.py:17
  27.1 71.7 %collective-permute-start.3 = (bf16[192,320]{0,1:T(8,128)(2,1)}, bf16[192,320]{0,1:T(8,128)(2,1)S(1)}, u32[]{:S(2)}, u32[]{:S(2)}) collective-permute-start(bf16[192,320]{0,1:T(8,128)(2,1)} %get-tuple-element.34), channel_id=1, source_target_pairs={{1,0},{0,1},{3,2},{2,3},{5,4},{4,5},{7,6},{6,7},{9,8},{8,9},{11,10... | collective-permute-start | bytes 368648 | tf_op jit(solution)/shard_map/ppermute | solution.py:17
  29.7 9.9 %copy-start.10 = (pred[128]{0:T(512)(128)(4,1)}, pred[128]{0:T(512)(128)(4,1)S(1)}, u32[]{:S(2)}) copy-start(pred[128]{0:T(512)(128)(4,1)S(1)} %compare_and_fusion.2) | copy-start | bytes 388
  30.3 9.4 %copy-start.7 = (s32[1024]{0:T(1024)}, s32[1024]{0:T(1024)S(1)}, u32[]{:S(2)}) copy-start(s32[1024]{0:T(1024)S(1)} %pad_clamp_fusion.1) | copy-start | bytes 12292
  31.2 7.0 %copy-start.4 = (f32[128,192]{1,0:T(8,128)}, f32[128,192]{1,0:T(8,128)S(1)}, u32[]{:S(2)}) copy-start(f32[128,192]{1,0:T(8,128)S(1)} %broadcast_select_fusion.13) | copy-start | bytes 294916
  31.2 5.1 %collective-permute-start.6 = (f32[2,192,32]{1,2,0:T(8,128)S(1)}, f32[2,192,32]{1,2,0:T(8,128)S(1)}, u32[]{:S(2)}, u32[]{:S(2)}) collective-permute-start(f32[2,192,32]{1,2,0:T(8,128)S(1)} %slice.192), channel_id=1, source_target_pairs={{1,0},{0,1},{3,2},{2,3},{5,4},{4,5},{7,6},{6,7},{9,8},{8,9},{11,10... | collective-permute-start | bytes 147464 | tf_op jit(solution)/shard_map/ppermute | solution.py:17
  36.3 1.9 copy-start.6
  36.9 3.6 %collective-permute-start.7 = (f32[192,32]{0,1:T(8,128)S(1)}, f32[192,32]{0,1:T(8,128)}, u32[]{:S(2)}, u32[]{:S(2)}) collective-permute-start(f32[192,32]{0,1:T(8,128)S(1)} %get-tuple-element.19), channel_id=1, source_target_pairs={{2,0},{4,2},{6,4},{8,6},{10,8},{12,10},{14,12},{16,14},{18,16},{20... | collective-permute-start | bytes 73736 | tf_op jit(solution)/shard_map/ppermute | solution.py:23
  41.3 49.2 %collective-permute-start.8 = (f32[192,32]{0,1:T(8,128)S(1)}, f32[192,32]{0,1:T(8,128)}, u32[]{:S(2)}, u32[]{:S(2)}) collective-permute-start(f32[192,32]{0,1:T(8,128)S(1)} %get-tuple-element.17), channel_id=1, source_target_pairs={{0,2},{2,4},{4,6},{6,8},{8,10},{10,12},{12,14},{14,16},{16,18},{18... | collective-permute-start | bytes 73736 | tf_op jit(solution)/shard_map/ppermute | solution.py:23
  90.5 9.1 %collective-permute-start.4 = (bf16[192,320]{0,1:T(8,128)(2,1)}, bf16[192,320]{0,1:T(8,128)(2,1)S(1)}, u32[]{:S(2)}, u32[]{:S(2)}) collective-permute-start(bf16[192,320]{0,1:T(8,128)(2,1)} %get-tuple-element.37), channel_id=1, source_target_pairs={{0,4},{2,6},{4,8},{6,10},{8,12},{10,14},{12,16},{14,18},{16,20},{1... | collective-permute-start | bytes 368648 | tf_op jit(solution)/shard_map/ppermute | solution.py:23
  94.7 7.4 %collective-permute-start.5 = (bf16[192,320]{0,1:T(8,128)(2,1)}, bf16[192,320]{0,1:T(8,128)(2,1)S(1)}, u32[]{:S(2)}, u32[]{:S(2)}) collective-permute-start(bf16[192,320]{0,1:T(8,128)(2,1)} %get-tuple-element.32), channel_id=1, source_target_pairs={{4,0},{6,2},{8,4},{10,6},{12,8},{14,10},{16,12},{18,14},{20,16},{2... | collective-permute-start | bytes 368648 | tf_op jit(solution)/shard_map/ppermute | solution.py:23
  96.0 7.6 %collective-permute-start.9 = (f32[2,192,32]{1,2,0:T(8,128)S(1)}, f32[2,192,32]{1,2,0:T(8,128)S(1)}, u32[]{:S(2)}, u32[]{:S(2)}) collective-permute-start(f32[2,192,32]{1,2,0:T(8,128)S(1)} %pad_maximum_fusion.2), channel_id=1, source_target_pairs={{1,0},{0,1},{3,2},{2,3},{5,4},{4,5},{7,6},{6,7},{9,8},{8,9},{11,10... | collective-permute-start | bytes 147464 | tf_op jit(solution)/shard_map/ppermute | solution.py:17
  98.9 5.5 %copy-start.8 = (f32[192]{0:T(256)S(1)}, f32[192]{0:T(256)}, u32[]{:S(2)}) copy-start(f32[192]{0:T(256)} %rsqrt_multiply_fusion.1) | copy-start | bytes 2308
  99.0 5.5 %copy-start.9 = (pred[128]{0:T(512)(128)(4,1)S(1)}, pred[128]{0:T(512)(128)(4,1)}, u32[]{:S(2)}) copy-start(pred[128]{0:T(512)(128)(4,1)} %compare_and_fusion.1) | copy-start | bytes 388
  102.3 1.3 copy-start.3
  115.5 1.3 copy-start
  133.6 2.7 %copy-start.11 = (pred[128]{0:T(512)(128)(4,1)S(1)}, pred[128]{0:T(512)(128)(4,1)}, u32[]{:S(2)}) copy-start(pred[128]{0:T(512)(128)(4,1)} %copy-done.10) | copy-start | bytes 388
  136.4 4.3 %collective-permute-start.16 = (f32[2,192,32]{1,2,0:T(8,128)S(1)}, f32[2,192,32]{1,2,0:T(8,128)S(1)}, u32[]{:S(2)}, u32[]{:S(2)}) collective-permute-start(f32[2,192,32]{1,2,0:T(8,128)S(1)} %slice.210), channel_id=1, source_target_pairs={{1,0},{0,1},{3,2},{2,3},{5,4},{4,5},{7,6},{6,7},{9,8},{8,9},{11,10... | collective-permute-start | bytes 147464 | tf_op jit(solution)/shard_map/ppermute | solution.py:17
  140.7 8.6 %collective-permute-start.17 = (f32[192,32]{0,1:T(8,128)S(1)}, f32[192,32]{0,1:T(8,128)S(1)}, u32[]{:S(2)}, u32[]{:S(2)}) collective-permute-start(f32[192,32]{0,1:T(8,128)S(1)} %get-tuple-element.13), channel_id=1, source_target_pairs={{2,0},{4,2},{6,4},{8,6},{10,8},{12,10},{14,12},{16,14},{18,16},{20... | collective-permute-start | bytes 73736 | tf_op jit(solution)/shard_map/ppermute | solution.py:23
  143.0 55.7 %collective-permute-start.10 = (bf16[192,320]{0,1:T(8,128)(2,1)}, bf16[192,320]{0,1:T(8,128)(2,1)S(1)}, u32[]{:S(2)}, u32[]{:S(2)}) collective-permute-start(bf16[192,320]{0,1:T(8,128)(2,1)} %get-tuple-element.29), channel_id=1, source_target_pairs={{0,2},{2,4},{4,6},{6,8},{8,10},{10,12},{12,14},{14,16},{16,18},{18... | collective-permute-start | bytes 368648 | tf_op jit(solution)/shard_map/ppermute | solution.py:23
  146.0 54.0 %collective-permute-start.11 = (bf16[192,320]{0,1:T(8,128)(2,1)}, bf16[192,320]{0,1:T(8,128)(2,1)S(1)}, u32[]{:S(2)}, u32[]{:S(2)}) collective-permute-start(bf16[192,320]{0,1:T(8,128)(2,1)} %get-tuple-element.30), channel_id=1, source_target_pairs={{2,0},{4,2},{6,4},{8,6},{10,8},{12,10},{14,12},{16,14},{18,16},{20... | collective-permute-start | bytes 368648 | tf_op jit(solution)/shard_map/ppermute | solution.py:23
  147.3 54.6 %collective-permute-start.12 = (bf16[192,320]{0,1:T(8,128)(2,1)}, bf16[192,320]{0,1:T(8,128)(2,1)S(1)}, u32[]{:S(2)}, u32[]{:S(2)}) collective-permute-start(bf16[192,320]{0,1:T(8,128)(2,1)} %get-tuple-element.27), channel_id=1, source_target_pairs={{1,0},{0,1},{3,2},{2,3},{5,4},{4,5},{7,6},{6,7},{9,8},{8,9},{11,10... | collective-permute-start | bytes 368648 | tf_op jit(solution)/shard_map/ppermute | solution.py:17
  148.4 53.4 %collective-permute-start.13 = (bf16[192,320]{0,1:T(8,128)(2,1)}, bf16[192,320]{0,1:T(8,128)(2,1)S(1)}, u32[]{:S(2)}, u32[]{:S(2)}) collective-permute-start(bf16[192,320]{0,1:T(8,128)(2,1)} %get-tuple-element.28), channel_id=1, source_target_pairs={{1,0},{0,1},{3,2},{2,3},{5,4},{4,5},{7,6},{6,7},{9,8},{8,9},{11,10... | collective-permute-start | bytes 368648 | tf_op jit(solution)/shard_map/ppermute | solution.py:17
  149.4 45.0 %collective-permute-start.18 = (f32[192,32]{0,1:T(8,128)S(1)}, f32[192,32]{0,1:T(8,128)S(1)}, u32[]{:S(2)}, u32[]{:S(2)}) collective-permute-start(f32[192,32]{0,1:T(8,128)S(1)} %get-tuple-element.11), channel_id=1, source_target_pairs={{0,2},{2,4},{4,6},{6,8},{8,10},{10,12},{12,14},{14,16},{16,18},{18... | collective-permute-start | bytes 73736 | tf_op jit(solution)/shard_map/ppermute | solution.py:23
  194.4 10.9 %collective-permute-start.14 = (bf16[192,320]{0,1:T(8,128)(2,1)}, bf16[192,320]{0,1:T(8,128)(2,1)S(1)}, u32[]{:S(2)}, u32[]{:S(2)}) collective-permute-start(bf16[192,320]{0,1:T(8,128)(2,1)} %get-tuple-element.31), channel_id=1, source_target_pairs={{0,4},{2,6},{4,8},{6,10},{8,12},{10,14},{12,16},{14,18},{16,20},{1... | collective-permute-start | bytes 368648 | tf_op jit(solution)/shard_map/ppermute | solution.py:23
  198.7 7.2 %collective-permute-start.15 = (bf16[192,320]{0,1:T(8,128)(2,1)S(1)}, bf16[192,320]{0,1:T(8,128)(2,1)S(1)}, u32[]{:S(2)}, u32[]{:S(2)}) collective-permute-start(bf16[192,320]{0,1:T(8,128)(2,1)S(1)} %get-tuple-element.26), channel_id=1, source_target_pairs={{4,0},{6,2},{8,4},{10,6},{12,8},{14,10},{16,12},{18,14},{20,16},{2... | collective-permute-start | bytes 368648 | tf_op jit(solution)/shard_map/ppermute | solution.py:23
  200.0 7.4 %collective-permute-start.19 = (f32[2,192,32]{1,2,0:T(8,128)S(1)}, f32[2,192,32]{1,2,0:T(8,128)S(1)}, u32[]{:S(2)}, u32[]{:S(2)}) collective-permute-start(f32[2,192,32]{1,2,0:T(8,128)S(1)} %pad_maximum_fusion.3), channel_id=1, source_target_pairs={{1,0},{0,1},{3,2},{2,3},{5,4},{4,5},{7,6},{6,7},{9,8},{8,9},{11,10... | collective-permute-start | bytes 147464 | tf_op jit(solution)/shard_map/ppermute | solution.py:17
  206.0 1.3 copy-start.2
  208.9 11.1 %copy-start.1 = (f32[192,2048]{0,1:T(8,128)S(1)}, f32[192,2048]{0,1:T(8,128)}, u32[]{:S(2)}) copy-start(f32[192,2048]{0,1:T(8,128)} %copy-done) | copy-start | bytes 4718596
where the time goes:
time: 227 us; the launch traced here: 226 us
  blocking collectives  81.7 us (36%)
  local copies, waits for them, and re-layouts  51.8 us (23%)
  starting transfers between devices  42.5 us (19%)
  other arithmetic  22.6 us (10%)
  matrix products  13.4 us (6%)
  waiting for transfers between devices  12.8 us (6%)
    psum x2, blocking collectives, local(): total_sq = lax.psum(squares - owned - edge_part, ('gx', 'gy'))  81.7 us
    ppermute x12, starting transfers between devices, passed_along(): return lax.ppermute(array, axis, pairs)  32.1 us
    scatter x2, local copies, waits for them, and re-layouts, local(): multipliers = multipliers + jnp.zeros_like(update).at[:, order].set(update)  21.4 us
    gather x2, local copies, waits for them, and re-layouts, local(): ordered = jnp.take(field, order, axis=1)  17.1 us
    dot_general x2, matrix products, local(): field = jnp.dot(rhs, flex, preferred_element_type=jnp.float32)  13.4 us
    ppermute x8, starting transfers between devices, shifted(): return lax.ppermute(block, axis, route)  10.3 us
    unnamed x28, local copies, waits for them, and re-layouts  8.23 us
    ppermute x12, waiting for transfers between devices, passed_along(): return lax.ppermute(array, axis, pairs)  7.77 us
  transfers between devices with their start and end apart: 20, of which 7 were waited for; matrix products, arithmetic and copies ran while one was open for 6% of the time, Pallas kernels for 0%

commit v1 on v0

v1 whole, which is shorter than its diff:
```python
import functools
import jax
import jax.numpy as jnp
from jax import lax
from jax.experimental import pallas as pl
from jax.experimental.pallas import tpu as pltpu
from jax.sharding import PartitionSpec as P

ITERS = 2
RHO = 0.2
RHO_CORNER = 0.5
EPS = 1e-06
MESH = pl.DeviceIdType.MESH
ROUNDS = ((0, 1, 0), (0, 1, 1), (1, 1, 0), (1, 1, 1), (0, 2, 0), (0, 2, 2))
PAIRS = (2, 0, 1)
F32 = jnp.float32
BF16 = jnp.bfloat16


def dot(a, b):
    return jnp.dot(a, b, preferred_element_type=F32)


def dot_nt(a, b):
    return lax.dot_general(a, b, (((1,), (1,)), ((), ())), preferred_element_type=F32)


def split(x):
    hi = x.astype(BF16)
    return hi, (x - hi.astype(F32)).astype(BF16)


def fold(x, low):
    h = x.shape[0] // 2
    lane = lax.broadcasted_iota(jnp.int32, (h, 128), 1)
    top, bottom = x[:h], x[h:]
    if low:
        return jnp.where(lane < 64, top, pltpu.roll(bottom, 64, 1))
    return jnp.where(lane < 64, pltpu.roll(top, 64, 1), bottom)


def unfold(low, high):
    h = low.shape[0]
    lane = lax.broadcasted_iota(jnp.int32, (h, 128), 1)
    top = jnp.where(lane < 64, low, pltpu.roll(high, 64, 1))
    bottom = jnp.where(lane < 64, pltpu.roll(low, 64, 1), high)
    return jnp.concatenate([top, bottom], axis=0)


def kernel(nx, ny, order_ref, ids_ref, loads_ref, flex_hbm, field_out, mult_out,
           flex, perm, permt, cperm, cpermt, fld, fhi, flo, rhs, mult, cmask,
           tb, rv, cs, cr, us, ur, sq, sr,
           flex_sem, tsend, trecv, csend, crecv, usend, urecv, ssend, srecv, osem):
    rows, n = loads_ref.shape
    face = (n - 128) // 6
    pair_w = 2 * face
    ncorn = ids_ref.shape[1]
    nf = 6 * face
    ix, iy = lax.axis_index("gx"), lax.axis_index("gy")
    ndev = nx * ny
    me = ix * ny + iy
    nch = flex_sem.shape[0]
    cw = n // nch

    def flex_copy(c):
        s = pl.ds(c * cw, cw)
        return pltpu.make_async_copy(flex_hbm.at[:, s], flex.at[:, s], flex_sem.at[c])

    for c in range(nch):
        flex_copy(c).start()

    def peer(k):
        p = lax.rem(me + k, ndev)
        return (p // ny, lax.rem(p, ny))

    barrier = pltpu.get_barrier_semaphore()

    def greet(k, carry):
        pl.semaphore_signal(barrier, inc=1, device_id=peer(k), device_id_type=MESH)
        return carry

    lax.fori_loop(1, ndev, greet, 0)

    partners = []
    for axis, dist, off in ROUNDS:
        idx = ix if axis == 0 else iy
        count = nx if axis == 0 else ny
        lower = lax.rem((idx - off + 2 * dist) // dist, 2) == 0
        to = jnp.where(lower, idx + dist, idx - dist)
        if axis == 0:
            partners.append((jnp.logical_and(to >= 0, to < count), (jnp.clip(to, 0, count - 1), iy)))
        else:
            partners.append((None, (ix, lax.rem(to + count, count))))

    for it in range(ITERS):
        for r in range(6):
            present = partners[r][0]
            if present is not None:
                @pl.when(jnp.logical_not(present))
                def _():
                    rv[it, r] = jnp.zeros(rv.shape[2:], BF16)
        @pl.when(ix == 0)
        def _():
            ur[it, 0] = jnp.zeros(ur.shape[2:], F32)
        @pl.when(ix == nx - 1)
        def _():
            ur[it, 1] = jnp.zeros(ur.shape[2:], F32)

    step_p = 64

    def build(b, carry):
        base = pl.multiple_of(b * step_p, step_p)
        row = lax.broadcasted_iota(jnp.int32, (step_p, n), 0) + base
        perm[pl.ds(base, step_p), :] = jnp.where(row == order_ref[...], 1.0, 0.0).astype(BF16)
        return carry

    lax.fori_loop(0, n // step_p, build, 0)
    ids = ids_ref[...]
    slot = ids // (ncorn // 4)
    moved = jnp.where(slot == 1, 2, jnp.where(slot == 2, 1, slot))
    ids = moved * (ncorn // 4) + lax.rem(ids, ncorn // 4)
    place = jnp.where(lax.broadcasted_iota(jnp.int32, (ncorn, ncorn), 0) == ids, 1.0, 0.0).astype(BF16)
    cperm[...] = dot_nt(perm[:, nf:], place).astype(BF16)

    def build_t():
        eye = (lax.broadcasted_iota(jnp.int32, (128, 128), 0)
               == lax.broadcasted_iota(jnp.int32, (128, 128), 1))

        def body(b, carry):
            base = pl.multiple_of(b * 128, 128)
            part = order_ref[:, pl.ds(base, 128)].astype(F32)
            col = jnp.sum(jnp.where(eye, part, 0.0), axis=1, keepdims=True).astype(jnp.int32)
            hit = lax.broadcasted_iota(jnp.int32, (128, n), 1) == col
            permt[pl.ds(base, 128), :] = jnp.where(hit, 1.0, 0.0).astype(BF16)
            return carry

        lax.fori_loop(0, n // 128, body, 0)
        ct = dot(place, permt[nf:, :])
        cpermt[...] = ct.astype(BF16)
        cmask[...] = RHO * (1.0 - jnp.sum(ct, axis=0, keepdims=True))

    lane = lax.broadcasted_iota(jnp.int32, (rows, 128), 1)
    inv_low = jnp.where(ix == nx - 1, 0.5, 0.25).astype(F32)
    inv_high = jnp.where(ix == 0, 0.5, 0.25).astype(F32)
    entries = ndev * ncorn

    for it in range(ITERS):
        for c in range(nch):
            if it == 0:
                flex_copy(c).wait()
            s = slice(c * cw, (c + 1) * cw)
            f = dot(loads_ref[...] if it == 0 else rhs[...], flex[:, s])
            fld[:, s] = f
            hi, lo = split(f)
            fhi[:, s] = hi
            flo[:, s] = lo
        if it == ITERS - 1:
            out_field = pltpu.make_async_copy(fld, field_out, osem.at[0])
            out_field.start()

        cs[it] = dot(fhi[...], cperm[...]) + dot(flo[...], cperm[...])
        if it == 0:
            pl.semaphore_wait(barrier, ndev - 1)
        ccopies = []
        for k, step in enumerate((-1, 1) if ny > 2 else (1,)):
            ccopies.append(pltpu.make_async_remote_copy(
                src_ref=cs.at[it], dst_ref=cr.at[it, k], send_sem=csend.at[it, k],
                recv_sem=crecv.at[it, k],
                device_id=(ix, lax.rem(iy + step + ny, ny)), device_id_type=MESH))
            ccopies[-1].start()

        def face_copy(r):
            return pltpu.make_async_remote_copy(
                src_ref=tb.at[it, r], dst_ref=rv.at[it, r], send_sem=tsend.at[it, r],
                recv_sem=trecv.at[it, r], device_id=partners[r][1], device_id_type=MESH)

        def on(r, action):
            if partners[r][0] is None:
                action(face_copy(r))
            else:
                @pl.when(partners[r][0])
                def _():
                    action(face_copy(r))

        def send_pair(p):
            base = p * pair_w
            t = dot(fhi[...], perm[:, base:base + pair_w])
            h = rows // 4
            for q in (1, 0):
                r = 2 * p + q
                tb[it, r, :rows, :] = t[:, q * 256:(q + 1) * 256].astype(BF16)
                tail = fold(t[:, 512:], q == 0).astype(BF16)
                tb[it, r, rows:, :128] = tail[:h]
                tb[it, r, rows:, 128:] = tail[h:]
                on(r, lambda c: c.start())

        for p in PAIRS:
            send_pair(p)

        for c in ccopies:
            c.wait_recv()
        own = cs[it]
        fromup, fromdown = cr[it, 0], cr[it, len(ccopies) - 1]
        w = own + jnp.where(lax.rem(lane, 64) < 32, pltpu.roll(fromup, 96, 1), pltpu.roll(fromdown, 32, 1))
        us[it, 0] = fold(w, True)
        us[it, 1] = fold(w, False)

        def side_copy(k):
            to = jnp.clip(ix + 1 if k == 0 else ix - 1, 0, nx - 1)
            return pltpu.make_async_remote_copy(
                src_ref=us.at[it, k], dst_ref=ur.at[it, k], send_sem=usend.at[it, k],
                recv_sem=urecv.at[it, k], device_id=(to, iy), device_id_type=MESH)

        @pl.when(ix < nx - 1)
        def _():
            side_copy(0).start()

        @pl.when(ix > 0)
        def _():
            side_copy(1).start()

        if it == 0:
            build_t()

        @pl.when(ix > 0)
        def _():
            side_copy(0).wait_recv()

        @pl.when(ix < nx - 1)
        def _():
            side_copy(1).wait_recv()

        cross = w + unfold(ur[it, 1], ur[it, 0])
        resid = own - cross * jnp.where(lane < 64, inv_low, inv_high)
        z = jnp.concatenate([resid * resid, jnp.zeros((256 - rows, 128), F32)], axis=0)
        part = jnp.sum(z.T, axis=0, keepdims=True)
        sq[it] = part

        def spread(k, carry):
            pltpu.make_async_remote_copy(
                src_ref=sq.at[it], dst_ref=sr.at[it, ndev - 1 - k], send_sem=ssend.at[it],
                recv_sem=srecv.at[it], device_id=peer(k), device_id_type=MESH).start()
            return carry

        lax.fori_loop(1, ndev, spread, 0)

        for c in range(nch):
            s = slice(c * cw, (c + 1) * cw)
            own_part = cmask[:, s] * fld[:, s]
            mult[:, s] = own_part if it == 0 else mult[:, s] + own_part

        def add_back(x, m):
            for c in range(nch):
                s = slice(c * cw, (c + 1) * cw)
                mult[:, s] += m(x, s)

        for p in PAIRS:
            for q in (1, 0):
                on(2 * p + q, lambda c: c.wait_recv())
            tails = []
            for q in (0, 1):
                r = 2 * p + q
                tails.append(jnp.concatenate([rv[it, r, rows:, :128], rv[it, r, rows:, 128:]], axis=0).astype(F32))
            x = jnp.concatenate(
                [rv[it, 2 * p, :rows, :], rv[it, 2 * p + 1, :rows, :], unfold(*tails).astype(BF16)], axis=1)
            base = p * pair_w
            add_back(x, lambda x, s: -RHO * dot(x, permt[base:base + pair_w, s]))

        pltpu.make_async_copy(sr.at[it], sr.at[it], srecv.at[it]).wait()
        total = part + jnp.sum(sr[it], axis=0)
        scale = RHO_CORNER / jnp.sqrt(total / entries + EPS)
        grid = jnp.broadcast_to(scale, (128, 256)).T[:rows]
        hi, lo = split(resid * grid)
        both = jnp.concatenate([hi, lo], axis=1)
        for c in range(nch):
            s = slice(c * cw, (c + 1) * cw)
            cp = cpermt[:, s]
            m = mult[:, s] + dot(both, jnp.concatenate([cp, cp], axis=0))
            mult[:, s] = m
            if it < ITERS - 1:
                rhs[:, s] = (loads_ref[:, s].astype(F32) - m).astype(BF16)

        for r in range(6):
            on(r, lambda c: c.wait_send())
        for c in ccopies:
            c.wait_send()

        @pl.when(ix < nx - 1)
        def _():
            side_copy(0).wait_send()

        @pl.when(ix > 0)
        def _():
            side_copy(1).wait_send()

        pltpu.make_async_copy(sr.at[it], sr.at[it], ssend.at[it]).wait()

    out_mult = pltpu.make_async_copy(mult, mult_out, osem.at[1])
    out_mult.start()
    out_field.wait()
    out_mult.wait()


def local(nx, ny, flexibility, loads, dof_order, coarse_ids):
    flex = flexibility[0, 0]
    load = loads[0, 0]
    order = dof_order[0]
    ids = coarse_ids[0]
    rows, n = load.shape
    corners = ids.shape[1]
    face = (n - corners) // 6
    ndev = nx * ny
    parts = []
    for p in range(3):
        a, b = 2 * p * face, (2 * p + 1) * face
        parts += [order[:, a:a + 256], order[:, b:b + 256],
                  order[:, a + 256:a + face], order[:, b + 256:b + face]]
    parts.append(order[:, 6 * face:])
    order = jnp.concatenate(parts, axis=1)
    vm = pl.BlockSpec(memory_space=pltpu.VMEM)
    hbm = pl.BlockSpec(memory_space=pl.ANY)
    sems = pltpu.SemaphoreType.DMA
    trace_rows = rows * face // 256
    ky = 2 if ny > 2 else 1
    out = jax.ShapeDtypeStruct((rows, n), F32)
    field, mult = pl.pallas_call(
        functools.partial(kernel, nx, ny),
        out_shape=(out, out),
        in_specs=[vm, vm, vm, hbm],
        out_specs=(hbm, hbm),
        scratch_shapes=[
            pltpu.VMEM((n, n), BF16), pltpu.VMEM((n, n), BF16), pltpu.VMEM((n, n), BF16),
            pltpu.VMEM((n, corners), BF16), pltpu.VMEM((corners, n), BF16),
            pltpu.VMEM((rows, n), F32), pltpu.VMEM((rows, n), BF16), pltpu.VMEM((rows, n), BF16),
            pltpu.VMEM((rows, n), BF16), pltpu.VMEM((rows, n), F32), pltpu.VMEM((1, n), F32),
            pltpu.VMEM((ITERS, 6, trace_rows, 256), BF16), pltpu.VMEM((ITERS, 6, trace_rows, 256), BF16),
            pltpu.VMEM((ITERS, rows, 128), F32), pltpu.VMEM((ITERS, ky, rows, 128), F32),
            pltpu.VMEM((ITERS, 2, rows // 2, 128), F32), pltpu.VMEM((ITERS, 2, rows // 2, 128), F32),
            pltpu.VMEM((ITERS, 1, 256), F32), pltpu.VMEM((ITERS, ndev - 1, 1, 256), F32),
            sems((4,)), sems((ITERS, 6)), sems((ITERS, 6)), sems((ITERS, ky)), sems((ITERS, ky)),
            sems((ITERS, 2)), sems((ITERS, 2)), sems((ITERS,)), sems((ITERS,)), sems((2,)),
        ],
        compiler_params=pltpu.CompilerParams(
            collective_id=0, has_side_effects=True, vmem_limit_bytes=60 * 1024 * 1024),
    )(order, ids, load, flex)
    return (field[None, None], mult[None, None])


def solution(mesh):
    nx, ny = mesh.shape["gx"], mesh.shape["gy"]
    placed = (
        P("gx", "gy", None, None),
        P("gx", "gy", None, None),
        P("gx", "gy", None),
        P("gx", "gy", None),
    )
    return jax.shard_map(
        functools.partial(local, nx, ny),
        mesh=mesh,
        in_specs=placed,
        out_specs=(P("gx", "gy", None, None), P("gx", "gy", None, None)),
        check_vma=False,
    )
```

time: 227 us -> 54.7 us (0.24)
  blocking collectives: 81.7 us -> 0 us
  Pallas kernels: 0 us -> 46.1 us
  local copies, waits for them, and re-layouts: 51.8 us -> 7.68 us
  starting transfers between devices: 42.5 us -> 0 us
  other arithmetic: 22.6 us -> 0 us
  matrix products: 13.4 us -> 0 us
  waiting for transfers between devices: 12.8 us -> 0 us
    psum x2 -> x0, blocking collectives: 81.7 us -> none  [local(): total_sq = lax.psum(squares - owned - edge_part, ('gx', 'gy'))]
    pallas_call x0 -> x1, Pallas kernels: none -> 46.1 us  [local(): pl.pallas_call(functools.partial(kernel, nx, ny), out_shape=(out, out), i...]
    ppermute x20 -> x0, starting transfers between devices: 42.5 us -> none  [the longest x12 32.1 us: passed_along(): return lax.ppermute(array, axis, pairs)]
    scatter x2 -> x0, local copies, waits for them, and re-layouts: 21.4 us -> none  [local(): multipliers = multipliers + jnp.zeros_like(update).at[:, order].set(update)]
    gather x6 -> x0, local copies, waits for them, and re-layouts: 20.3 us -> none  [the longest x2 17.1 us: local(): ordered = jnp.take(field, order, axis=1)]
    dot_general x2 -> x0, matrix products: 13.4 us -> none  [local(): field = jnp.dot(rhs, flex, preferred_element_type=jnp.float32)]
    ppermute x20 -> x0, waiting for transfers between devices: 12.8 us -> none  [the longest x12 7.77 us: passed_along(): return lax.ppermute(array, axis, pairs)]
    unnamed x28 -> x4, local copies, waits for them, and re-layouts: 8.23 us -> 3.97 us
  transfers between devices with their start and end apart: 20 -> 0, of which waited for: 7 -> 0; matrix products, arithmetic and copies ran while one was open for 6% -> 0% of each run, Pallas kernels for 0% -> 0%
where the time goes in v1:
time: 54.7 us; the launch traced here: 54.4 us
  Pallas kernels  46.1 us (84%)
  local copies, waits for them, and re-layouts  7.68 us (14%)
  between operations  0.65 us (1%)
    pallas_call x1, Pallas kernels, local(): pl.pallas_call(functools.partial(kernel, nx, ny), out_shape=(out, out), i...  46.1 us
    unnamed x4, local copies, waits for them, and re-layouts  3.97 us
    slice x2, local copies, waits for them, and re-layouts, local(): order[:, b + 256:b + face]  1.52 us

profile of v1, /device:TPU:0, one launch (start us, length us, event | category | flops | bytes accessed | tf_op | source)
XLA Modules:
  0.0 54.4 jit_solution(4965524365693263482)
XLA Ops:
  0.6 0.8 %slice.55 = s32[1,192]{1,0:T(1,128)S(1)} slice(s32[1,2048]{1,0:T(1,128)} %bitcast.10), slice={[0:1], [1856:2048]} | slice | bytes 1536 | tf_op jit(solution)/shard_map/slice | solution.py:317
  1.4 0.7 %fusion = (s32[1,64]{1,0:T(1,128)S(1)}, s32[1,64]{1,0:T(1,128)S(1)}, s32[1,64]{1,0:T(1,128)S(1)}) fusion(s32[1,2048]{1,0:T(1,128)} %bitcast.11), kind=kLoop, calls=%fused_computation | loop fusion | bytes 1536 | tf_op jit(solution)/shard_map/slice | solution.py:317
  2.1 0.8 %fusion.2 = (s32[1,320]{1,0:T(1,128)S(1)}, s32[1,320]{1,0:T(1,128)S(1)}) fusion(s32[1,2048]{1,0:T(1,128)} %bitcast.12), kind=kLoop, calls=%fused_computation.2 | loop fusion | bytes 5120 | tf_op jit(solution)/shard_map/slice | solution.py:317
  2.8 0.8 %fusion.1 = (s32[1,256]{1,0:T(1,128)S(1)}, s32[1,256]{1,0:T(1,128)S(1)}, s32[1,256]{1,0:T(1,128)S(1)}, s32[1,256]{1,0:T(1,128)S(1)}) fusion(s32[1,2048]{1,0:T(1,128)} %bitcast.13), kind=kLoop, calls=%fused_computation.1 | loop fusion | bytes 8192 | tf_op jit(solution)/shard_map/slice | solution.py:316
  3.6 0.7 %concatenate.3.order_ref = s32[1,2048]{1,0:T(1,128)} concatenate(s32[1,256]{1,0:T(1,128)S(1)} %get-tuple-element.12, s32[1,256]{1,0:T(1,128)S(1)} %get-tuple-element.11, s32[1,64]{1,0:T(1,128)S(1)} %get-tuple-element.8, s32[1,320]{1,0:T(1,128)S(1)} %get-tuple-element.14, s32[1,256]{1,0:T(1,128)S(1)} %get-tuple-element.10, s32[1,64]{1,0:T(1,128)S(1)} %get-tuple-element.7, ...), dimensions={1} | concatenate | bytes 16384 | tf_op jit(solution)/shard_map/concatenate | solution.py:319
  4.3 46.1 %shard_map.59 = (f32[192,2048]{1,0:T(8,128)}, f32[192,2048]{1,0:T(8,128)}) custom-call(s32[1,2048]{1,0:T(1,128)} %concatenate.3.order_ref, s32[1,128]{1,0:T(1,128)} %bitcast.14, bf16[192,2048]{1,0:T(8,128)(2,1)} %bitcast.9, bf16[2048,2048]{1,0:T(8,128)(2,1)} %bitcast.6), custom_call_target="tpu_custom_call" | custom-call | tf_op jit(solution)/shard_map/pallas_call | solution.py:326
  50.5 0.0 copy-start
  50.5 2.8 %copy.8 = f32[1,1,192,2048]{3,2,1,0:T(8,128)} copy(f32[1,1,192,2048]{3,2,1,0:T(8,128)} %bitcast.8) | data formatting | bytes 3145728
  53.3 0.0 copy-done
  53.3 1.1 %copy.9 = f32[1,1,192,2048]{3,2,1,0:T(8,128)} copy(f32[1,1,192,2048]{3,2,1,0:T(8,128)S(1)} %bitcast.7) | data formatting | bytes 3145728
Async XLA Ops:
  50.5 2.8 %copy-start = (f32[192,2048]{1,0:T(8,128)S(1)}, f32[192,2048]{1,0:T(8,128)}, u32[]{:S(2)}) copy-start(f32[192,2048]{1,0:T(8,128)} %get-tuple-element.5) | copy-start | bytes 4718596

commit v2 on v1

--- a/solution.py
+++ b/solution.py
@@ -13,6 +13,7 @@
 MESH = pl.DeviceIdType.MESH
 ROUNDS = ((0, 1, 0), (0, 1, 1), (1, 1, 0), (1, 1, 1), (0, 2, 0), (0, 2, 2))
 PAIRS = (2, 0, 1)
+BACK = (1, 0, 2)
 F32 = jnp.float32
 BF16 = jnp.bfloat16
 
@@ -48,7 +49,7 @@
 
 
 def kernel(nx, ny, order_ref, ids_ref, loads_ref, flex_hbm, field_out, mult_out,
-           flex, perm, permt, cperm, cpermt, fld, fhi, flo, rhs, mult, cmask,
+           order, flex, perm, permt, cperm, cpermt, fld, fhi, flo, rhs, mult, cmask,
            tb, rv, cs, cr, us, ur, sq, sr,
            flex_sem, tsend, trecv, csend, crecv, usend, urecv, ssend, srecv, osem):
     rows, n = loads_ref.shape
@@ -106,12 +107,21 @@
         def _():
             ur[it, 1] = jnp.zeros(ur.shape[2:], F32)
 
+    for p in range(3):
+        base = p * pair_w
+        x = jnp.broadcast_to(order_ref[:, base:base + pair_w], (8, pair_w))
+        turned = pltpu.roll(x, pair_w - 64, 1)
+        low = lax.broadcasted_iota(jnp.int32, (8, 128), 1) < 64
+        order[:, base:base + 256] = x[:, :256]
+        order[:, base + 256:base + 512] = turned[:, 256:512]
+        order[:, base + 512:base + pair_w] = jnp.where(low, x[:, 256:384], x[:, 512:])
+    order[:, nf:] = jnp.broadcast_to(order_ref[:, nf:], (8, ncorn))
     step_p = 64
 
     def build(b, carry):
         base = pl.multiple_of(b * step_p, step_p)
         row = lax.broadcasted_iota(jnp.int32, (step_p, n), 0) + base
-        perm[pl.ds(base, step_p), :] = jnp.where(row == order_ref[...], 1.0, 0.0).astype(BF16)
+        perm[pl.ds(base, step_p), :] = jnp.where(row == order[0:1, :], 1.0, 0.0).astype(BF16)
         return carry
 
     lax.fori_loop(0, n // step_p, build, 0)
@@ -128,7 +138,7 @@
 
         def body(b, carry):
             base = pl.multiple_of(b * 128, 128)
-            part = order_ref[:, pl.ds(base, 128)].astype(F32)
+            part = order[0:1, pl.ds(base, 128)].astype(F32)
             col = jnp.sum(jnp.where(eye, part, 0.0), axis=1, keepdims=True).astype(jnp.int32)
             hit = lax.broadcasted_iota(jnp.int32, (128, n), 1) == col
             permt[pl.ds(base, 128), :] = jnp.where(hit, 1.0, 0.0).astype(BF16)
@@ -222,6 +232,11 @@
         if it == 0:
             build_t()
 
+        for c in range(nch):
+            s = slice(c * cw, (c + 1) * cw)
+            own_part = cmask[:, s] * fld[:, s]
+            mult[:, s] = own_part if it == 0 else mult[:, s] + own_part
+
         @pl.when(ix > 0)
         def _():
             side_copy(0).wait_recv()
@@ -244,17 +259,12 @@
 
         lax.fori_loop(1, ndev, spread, 0)
 
-        for c in range(nch):
-            s = slice(c * cw, (c + 1) * cw)
-            own_part = cmask[:, s] * fld[:, s]
-            mult[:, s] = own_part if it == 0 else mult[:, s] + own_part
-
         def add_back(x, m):
             for c in range(nch):
                 s = slice(c * cw, (c + 1) * cw)
                 mult[:, s] += m(x, s)
 
-        for p in PAIRS:
+        for p in BACK:
             for q in (1, 0):
                 on(2 * p + q, lambda c: c.wait_recv())
             tails = []
@@ -304,19 +314,11 @@
 def local(nx, ny, flexibility, loads, dof_order, coarse_ids):
     flex = flexibility[0, 0]
     load = loads[0, 0]
-    order = dof_order[0]
     ids = coarse_ids[0]
     rows, n = load.shape
     corners = ids.shape[1]
     face = (n - corners) // 6
     ndev = nx * ny
-    parts = []
-    for p in range(3):
-        a, b = 2 * p * face, (2 * p + 1) * face
-        parts += [order[:, a:a + 256], order[:, b:b + 256],
-                  order[:, a + 256:a + face], order[:, b + 256:b + face]]
-    parts.append(order[:, 6 * face:])
-    order = jnp.concatenate(parts, axis=1)
     vm = pl.BlockSpec(memory_space=pltpu.VMEM)
     hbm = pl.BlockSpec(memory_space=pl.ANY)
     sems = pltpu.SemaphoreType.DMA
@@ -329,6 +331,7 @@
         in_specs=[vm, vm, vm, hbm],
         out_specs=(hbm, hbm),
         scratch_shapes=[
+            pltpu.VMEM((8, n), jnp.int32),
             pltpu.VMEM((n, n), BF16), pltpu.VMEM((n, n), BF16), pltpu.VMEM((n, n), BF16),
             pltpu.VMEM((n, corners), BF16), pltpu.VMEM((corners, n), BF16),
             pltpu.VMEM((rows, n), F32), pltpu.VMEM((rows, n), BF16), pltpu.VMEM((rows, n), BF16),
@@ -341,8 +344,8 @@
             sems((ITERS, 2)), sems((ITERS, 2)), sems((ITERS,)), sems((ITERS,)), sems((2,)),
         ],
         compiler_params=pltpu.CompilerParams(
-            collective_id=0, has_side_effects=True, vmem_limit_bytes=60 * 1024 * 1024),
-    )(order, ids, load, flex)
+            collective_id=0, has_side_effects=True, vmem_limit_bytes=44 * 1024 * 1024),
+    )(dof_order[0], ids, load, flex)
     return (field[None, None], mult[None, None])
 
 

time: 54.7 us -> 50.1 us (0.916)
  local copies, waits for them, and re-layouts: 7.68 us -> 4.76 us
  Pallas kernels: 46.1 us -> 44.4 us
    slice x4 -> x0, local copies, waits for them, and re-layouts: 3.02 us -> none  [the longest x2 1.52 us: local(): order[:, b + 256:b + face]]
    pallas_call x1, Pallas kernels: 46.1 us -> 44.4 us  [local(): pl.pallas_call(functools.partial(kernel, nx, ny), out_shape=(out, out), i...]
    unnamed x4 -> x8, local copies, waits for them, and re-layouts: 3.97 us -> 4.76 us
    concatenate x1 -> x0, local copies, waits for them, and re-layouts: 0.7 us -> none  [local(): order = jnp.concatenate(parts, axis=1)]
where the time goes in v2:
time: 50.1 us; the launch traced here: 49.8 us
  Pallas kernels  44.4 us (89%)
  local copies, waits for them, and re-layouts  4.76 us (10%)
  between operations  0.65 us (1%)
    pallas_call x1, Pallas kernels, local(): pl.pallas_call(functools.partial(kernel, nx, ny), out_shape=(out, out), i...  44.4 us
    unnamed x8, local copies, waits for them, and re-layouts  4.76 us

profile of v2, /device:TPU:0, one launch (start us, length us, event | category | flops | bytes accessed | tf_op | source)
XLA Modules:
  0.0 49.8 jit_solution(15803216433748388442)
XLA Ops:
  0.6 0.0 copy-start
  0.6 1.1 %copy-done = bf16[1,1,192,2048]{3,2,1,0:T(8,128)(2,1)S(1)} copy-done((bf16[1,1,192,2048]{3,2,1,0:T(8,128)(2,1)S(1)}, bf16[1,1,192,2048]{3,2,1,0:T(8,128)(2,1)}, u32[]{:S(2)}) %copy-start) | copy-done | bytes 786456
  1.8 0.0 copy-start.1
  1.8 0.7 %copy-done.1 = s32[1,1,2048]{2,1,0:T(1,128)S(1)} copy-done((s32[1,1,2048]{2,1,0:T(1,128)S(1)}, s32[1,1,2048]{2,1,0:T(1,128)}, u32[]{:S(2)}) %copy-start.1) | copy-done | bytes 8216
  2.5 0.0 copy-start.2
  2.5 0.7 %copy-done.2 = s32[1,1,128]{2,1,0:T(1,128)S(1)} copy-done((s32[1,1,128]{2,1,0:T(1,128)S(1)}, s32[1,1,128]{2,1,0:T(1,128)}, u32[]{:S(2)}) %copy-start.2) | copy-done | bytes 536
  3.1 44.4 %shard_map.59 = (f32[192,2048]{1,0:T(8,128)S(1)}, f32[192,2048]{1,0:T(8,128)S(1)}) custom-call(s32[1,2048]{1,0:T(1,128)S(1)} %bitcast.9, s32[1,128]{1,0:T(1,128)S(1)} %bitcast.10, bf16[192,2048]{1,0:T(8,128)(2,1)S(1)} %bitcast.8, bf16[2048,2048]{1,0:T(8,128)(2,1)} %bitcast.11), custom_call_target="tpu_custom_call" | custom-call | tf_op jit(solution)/shard_map/pallas_call | solution.py:328
  47.6 1.1 %copy.8 = f32[1,1,192,2048]{3,2,1,0:T(8,128)} copy(f32[1,1,192,2048]{3,2,1,0:T(8,128)S(1)} %bitcast.7) | data formatting | bytes 3145728
  48.7 1.1 %copy.9 = f32[1,1,192,2048]{3,2,1,0:T(8,128)} copy(f32[1,1,192,2048]{3,2,1,0:T(8,128)S(1)} %bitcast.6) | data formatting | bytes 3145728
Async XLA Ops:
  0.6 1.1 %copy-start = (bf16[1,1,192,2048]{3,2,1,0:T(8,128)(2,1)S(1)}, bf16[1,1,192,2048]{3,2,1,0:T(8,128)(2,1)}, u32[]{:S(2)}) copy-start(bf16[1,1,192,2048]{3,2,1,0:T(8,128)(2,1)} %param.5) | copy-start | bytes 2359300
  1.8 0.7 %copy-start.1 = (s32[1,1,2048]{2,1,0:T(1,128)S(1)}, s32[1,1,2048]{2,1,0:T(1,128)}, u32[]{:S(2)}) copy-start(s32[1,1,2048]{2,1,0:T(1,128)} %param.6) | copy-start | bytes 24580
  2.5 0.7 %copy-start.2 = (s32[1,1,128]{2,1,0:T(1,128)S(1)}, s32[1,1,128]{2,1,0:T(1,128)}, u32[]{:S(2)}) copy-start(s32[1,1,128]{2,1,0:T(1,128)} %param.7) | copy-start | bytes 1540
